TPU v7x, 256 devices: a whole 4x4x8 slice. The times are simulated.
256 devices in a mesh: rows: 32 (over z_lo, x, core), sub: 8 (over y, z_hi).
Axes of the slice: x: 4, y: 4, z: 8 (z_hi: 2, z_lo: 4; z = z_hi * 4 + z_lo), core: 2. Of those that a mesh axis runs over, the one named last changes fastest.
Arguments:
- embeddings: bfloat16 [16384, 1024], P('rows', 'sub'), may hold values from -40 to 40
- rotation: bfloat16 [1024, 1024], P(None, 'sub'), may hold values from -0.1875 to 0.1875
- codebooks: float32 [64, 16, 256], P('sub'), may hold values from -6 to 6
Outputs:
- new_codebooks: float32 [64, 16, 256], P('sub')
- new_rotation: float32 [1024, 1024], P('rows', 'sub')
All inputs are finite; a program needn't handle non-finite values.
Results may differ from a plain program's by a relative error of at most 0.006.
The roundings to bfloat16 on the way count: a program that leaves them out, or rounds other values in their place, can miss the bound.
Values may be sent and summed in bfloat16 or wider, within the bound.
No kernel may reach another device: no remote copies, remote signals or barrier semaphores. Data moves between devices by JAX's collectives and lax.ppermute only.
A program may use at most 64 MiB of HBM per device.

v0:
```python
import jax
import jax.numpy as jnp
from jax import lax
from jax.sharding import PartitionSpec as P

SUB_DIM = 16
ITERS = 2
POLAR_ITER_COUNT = 2
softness_level = 4.0
prior_weight = 8.0
quintic_one = 3.4445
quintic_three = -4.775
quintic_five = 2.0315


def complete_feature_rows(embeddings):
    return lax.all_gather(embeddings, "sub", axis=1, tiled=True)


def subspace_pass(pieces, centroid_tables):
    books_low = centroid_tables.astype(jnp.bfloat16)

    def per_subspace(inputs):
        features, assignment_probs, codes_low = inputs
        cross_products = lax.dot_general(
            codes_low, features, (((0,), (0,)), ((), ())), preferred_element_type=jnp.float32
        )
        centroid_logits = (
            2.0 * cross_products - jnp.sum(assignment_probs * assignment_probs, axis=0)[:, None]
        ) / softness_level
        centroid_logits = centroid_logits - jnp.max(centroid_logits, axis=0, keepdims=True)
        exponent = jnp.exp(centroid_logits)
        weights = (exponent / jnp.sum(exponent, axis=0, keepdims=True)).astype(jnp.bfloat16)
        counts = jnp.sum(weights, axis=1, dtype=jnp.float32)
        totals = lax.dot_general(
            features, weights, (((1,), (1,)), ((), ())), preferred_element_type=jnp.float32
        )
        return (counts, totals, weights)

    return lax.map(per_subspace, (pieces, centroid_tables, books_low))


def per_device(embeddings, rotation, codebooks):
    row_count = embeddings.shape[0]
    width_own = rotation.shape[1]
    local_subs = codebooks.shape[0]
    full_x = complete_feature_rows(embeddings)
    rotated = lax.dot_general(
        rotation, full_x, (((0,), (1,)), ((), ())), preferred_element_type=jnp.float32
    ).astype(jnp.bfloat16)
    pieces = rotated.reshape(local_subs, SUB_DIM, row_count)
    books_now = codebooks
    weights = None
    for repeat in range(ITERS):
        counts, totals, weights = subspace_pass(pieces, books_now)
        totals, counts = lax.psum((totals, counts), "rows")
        books_now = (totals + prior_weight * books_now) / (counts[:, None, :] + prior_weight)
    books_low = books_now.astype(jnp.bfloat16)
    rebuilt = jnp.einsum("mdk,mkr->mdr", books_low, weights, preferred_element_type=jnp.float32)
    rebuilt = rebuilt.reshape(width_own, row_count).astype(jnp.bfloat16)
    row_share = full_x.shape[1] // lax.axis_size("rows")
    partial_value = lax.dot_general(
        full_x, rebuilt, (((0,), (1,)), ((), ())), preferred_element_type=jnp.float32
    )
    summed = lax.psum(partial_value, "rows")
    own_cross = lax.dynamic_slice_in_dim(summed, lax.axis_index("rows") * row_share, row_share, 0)
    frob_norm = jnp.sqrt(lax.psum(jnp.sum(own_cross * own_cross), ("rows", "sub")) + 1e-06)
    polar_now = own_cross / frob_norm
    for polar_rotation_step in range(POLAR_ITER_COUNT):
        columns = lax.all_gather(polar_now, "rows", axis=0, tiled=True)
        gram_part = lax.dot_general(
            polar_now,
            columns,
            (((1,), (1,)), ((), ())),
            precision=lax.Precision.HIGHEST,
            preferred_element_type=jnp.float32,
        )
        gram_rows = lax.psum(gram_part, "sub")
        image = jnp.dot(
            gram_rows, columns, precision=lax.Precision.HIGHEST, preferred_element_type=jnp.float32
        )
        image_cols = lax.all_gather(image, "rows", axis=0, tiled=True)
        second = jnp.dot(
            gram_rows,
            image_cols,
            precision=lax.Precision.HIGHEST,
            preferred_element_type=jnp.float32,
        )
        polar_now = quintic_one * polar_now + quintic_three * image + quintic_five * second
    return (books_now, polar_now)


def solution(mesh):
    return jax.shard_map(
        per_device,
        mesh=mesh,
        in_specs=(P("rows", "sub"), P(None, "sub"), P("sub", None, None)),
        out_specs=(P("sub", None, None), P("rows", "sub")),
        check_vma=False,
    )
```

profile of v0, /device:TPU:1, one launch (start us, length us, event | category | flops | bytes accessed | tf_op | source)
XLA Modules:
  0.0 1482.6 jit_solution(5863832114635413068)
XLA Ops:
  8.0 0.9 convert_element_type.30
  8.9 65.7 %all-gather.2.cloned.1.call-done = bf16[512,1024]{1,0:T(8,128)(2,1)} async-done(((bf16[512,128]{1,0:T(8,128)(2,1)}), bf16[512,1024]{1,0:T(8,128)(2,1)}) %all-gather.2.cloned.1.call-update) | async-done | bytes 1048592 | tf_op jit(solution)/shard_map/all_gather | solution.py:17
  74.6 1.7 convolution_convert_fusion.1
  76.4 12.3 while.26
  88.7 69.8 %psum.57 = f32[8,256]{1,0:T(8,128)S(1)} all-reduce(f32[8,256]{1,0:T(8,128)S(1)} %get-tuple-element.75), channel_id=1, replica_groups=mesh['rows'=32,'sub'=8] {'rows'}, use_global_device_ids=true, to_apply=%region_7.8 | all-reduce | flops 2048 | bytes 16384 | tf_op jit(solution)/shard_map/psum | solution.py:56
  158.6 247.6 %all-reduce.6.cloned.1.call-done = f32[8,16,256]{2,1,0:T(8,128)} async-done(((f32[8,16,256]{2,1,0:T(8,128)}), f32[8,16,256]{2,1,0:T(8,128)}) %all-reduce.6.cloned.1.call-update) | async-done | bytes 131088 | tf_op jit(solution)/shard_map/psum | solution.py:56
  406.1 1.0 fusion.27
  407.8 11.8 while.27
  408.3 0.8 fusion.72
  409.8 0.8 fusion.72
  412.7 0.8 fusion.72
  414.2 0.8 fusion.72
  418.7 0.8 fusion.72
  419.6 70.0 %psum.59 = f32[8,256]{1,0:T(8,128)S(1)} all-reduce(f32[8,256]{1,0:T(8,128)S(1)} %get-tuple-element.77), channel_id=1, replica_groups=mesh['rows'=32,'sub'=8] {'rows'}, use_global_device_ids=true, to_apply=%region_15.16 | all-reduce | flops 2048 | bytes 16384 | tf_op jit(solution)/shard_map/psum | solution.py:56
  489.7 252.1 %all-reduce.8.cloned.1.call-done = f32[8,16,256]{2,1,0:T(8,128)} async-done(((f32[8,16,256]{2,1,0:T(8,128)}), f32[8,16,256]{2,1,0:T(8,128)}) %all-reduce.8.cloned.1.call-update) | async-done | bytes 131088 | tf_op jit(solution)/shard_map/psum | solution.py:56
  741.8 0.9 add_divide_fusion
  743.4 1.4 convolution_bitcast_fusion.2
  744.8 275.9 %all-reduce.10.cloned.1.call-done = f32[1024,128]{1,0:T(8,128)} async-done(((f32[1024,128]{1,0:T(8,128)}), f32[1024,128]{1,0:T(8,128)}) %all-reduce.10.cloned.1.call-update) | async-done | bytes 524304 | tf_op jit(solution)/shard_map/psum | solution.py:65
  1020.8 1.3 multiply_reduce_fusion.2
  1022.1 78.1 %psum.61 = f32[]{:T(128)} all-reduce(f32[]{:T(128)} %multiply_reduce_fusion.2), channel_id=1, replica_groups=mesh['rows'=32,'sub'=8] {'rows','sub'}, use_global_device_ids=true, to_apply=%region_18.19 | all-reduce | flops 1 | bytes 8 | tf_op jit(solution)/shard_map/psum | solution.py:67
  1101.6 39.9 %all_gather.16 = f32[1024,128]{1,0:T(8,128)S(1)} all-gather(f32[32,128]{1,0:T(8,128)S(1)} %dynamic-slice_divide_fusion), channel_id=1, replica_groups=mesh['rows'=32,'sub'=8] {'rows'}, dimensions={0}, use_global_device_ids=true | all-gather | bytes 540672 | tf_op jit(solution)/shard_map/all_gather | solution.py:70
  1141.5 1.3 fusion.30
  1142.8 95.5 %all-reduce.12.cloned.1.call-done = f32[32,1024]{1,0:T(8,128)} async-done(((f32[32,1024]{1,0:T(8,128)}), f32[32,1024]{1,0:T(8,128)}) %all-reduce.12.cloned.1.call-update) | async-done | bytes 131088 | tf_op jit(solution)/shard_map/psum | solution.py:78
  1238.3 1.3 fusion.31
  1239.6 47.8 %all_gather.17 = f32[1024,128]{1,0:T(8,128)S(1)} all-gather(f32[32,128]{1,0:T(8,128)S(1)} %fusion.31), channel_id=1, replica_groups=mesh['rows'=32,'sub'=8] {'rows'}, dimensions={0}, use_global_device_ids=true | all-gather | bytes 540672 | tf_op jit(solution)/shard_map/all_gather | solution.py:82
  1287.5 1.3 fusion.25
  1288.8 39.3 %all_gather.18 = f32[1024,128]{1,0:T(8,128)S(1)} all-gather(f32[32,128]{1,0:T(8,128)S(1)} %fusion.25), channel_id=1, replica_groups=mesh['rows'=32,'sub'=8] {'rows'}, dimensions={0}, use_global_device_ids=true | all-gather | bytes 540672 | tf_op jit(solution)/shard_map/all_gather | solution.py:70
  1328.1 1.3 fusion.32
  1329.3 95.4 %all-reduce.14.cloned.1.call-done = f32[32,1024]{1,0:T(8,128)} async-done(((f32[32,1024]{1,0:T(8,128)}), f32[32,1024]{1,0:T(8,128)}) %all-reduce.14.cloned.1.call-update) | async-done | bytes 131088 | tf_op jit(solution)/shard_map/psum | solution.py:78
  1424.7 1.3 fusion.33
  1426.0 47.8 %all_gather.19 = f32[1024,128]{1,0:T(8,128)S(1)} all-gather(f32[32,128]{1,0:T(8,128)S(1)} %fusion.33), channel_id=1, replica_groups=mesh['rows'=32,'sub'=8] {'rows'}, dimensions={0}, use_global_device_ids=true | all-gather | bytes 540672 | tf_op jit(solution)/shard_map/all_gather | solution.py:82
  1473.9 1.9 fusion.24
  (128 shorter events, 22.7 us)
Async XLA Ops:
  7.2 67.5 %copy-start = (bf16[1024,128]{1,0:T(8,128)(2,1)S(1)}, bf16[1024,128]{1,0:T(8,128)(2,1)}, u32[]{:S(2)}) copy-start(bf16[1024,128]{1,0:T(8,128)(2,1)} %param.8) | copy-start | bytes 786436
  7.2 67.5 %all-gather.2.cloned.1.call-start = ((), (), s32[]{:S(2)}) async-start(), calls=%async_computation | async-start | bytes 1179648 | tf_op jit(solution)/shard_map/all_gather | solution.py:17
  7.9 398.2 %all-reduce.6.cloned.1.call-start = ((), (), s32[]{:S(2)}) async-start(), calls=%async_computation.1 | async-start | bytes 262144 | tf_op jit(solution)/shard_map/psum | solution.py:56
  88.7 69.8 %copy-start.3 = (f32[8,16,256]{2,1,0:T(8,128)}, f32[8,16,256]{2,1,0:T(8,128)S(1)}, u32[]{:S(2)}) copy-start(f32[8,16,256]{2,1,0:T(8,128)S(1)} %get-tuple-element.74) | copy-start | bytes 393220
  158.5 583.3 %all-reduce.8.cloned.1.call-start = ((), (), s32[]{:S(2)}) async-start(), calls=%async_computation.2 | async-start | bytes 262144 | tf_op jit(solution)/shard_map/psum | solution.py:56
  419.6 323.8 %copy-start.1 = (bf16[512,1024]{1,0:T(8,128)(2,1)S(1)}, bf16[512,1024]{1,0:T(8,128)(2,1)}, u32[]{:S(2)}) copy-start(bf16[512,1024]{1,0:T(8,128)(2,1)} %all-gather.2.cloned.1.call-done) | copy-start | bytes 3145732
  489.7 531.1 %all-reduce.10.cloned.1.call-start = ((), (), s32[]{:S(2)}) async-start(), calls=%async_computation.3 | async-start | bytes 1048576 | tf_op jit(solution)/shard_map/psum | solution.py:65
  742.7 0.7 copy-start.2
  744.8 493.5 %all-reduce.12.cloned.1.call-start = ((), (), s32[]{:S(2)}) async-start(), calls=%async_computation.4 | async-start | bytes 262144 | tf_op jit(solution)/shard_map/psum | solution.py:78
  1142.8 282.0 %all-reduce.14.cloned.1.call-start = ((), (), s32[]{:S(2)}) async-start(), calls=%async_computation.5 | async-start | bytes 262144 | tf_op jit(solution)/shard_map/psum | solution.py:78
Sparse Core Ops, SparseCore 0:
  10.5 64.1 all-gather.1
  158.6 247.4 all-reduce.5
  489.8 251.9 all-reduce.7
  744.9 275.8 all-reduce.9
  1142.9 95.3 all-reduce.11
  1329.5 95.2 all-reduce.13
where the time goes:
time: 1480 us
  waiting for transfers between devices  1030 us (70%)
  blocking collectives  393 us (27%)
  matrix products  23.6 us (2%)
  other arithmetic  15.8 us (1%)
  between operations  15 us (1%)
    psum x2, waiting for transfers between devices, per_device(): totals, counts = lax.psum((totals, counts), 'rows')  500 us
    psum x1, waiting for transfers between devices, per_device(): summed = lax.psum(partial_value, 'rows')  276 us
    psum x2, waiting for transfers between devices, per_device(): gram_rows = lax.psum(gram_part, 'sub')  191 us
    psum x2, blocking collectives, per_device(): totals, counts = lax.psum((totals, counts), 'rows')  140 us
    all_gather x2, blocking collectives, per_device(): image_cols = lax.all_gather(image, 'rows', axis=0, tiled=True)  95.7 us
    all_gather x2, blocking collectives, per_device(): columns = lax.all_gather(polar_now, 'rows', axis=0, tiled=True)  79.2 us
    psum x1, blocking collectives, per_device(): lax.psum(jnp.sum(own_cross * own_cross), ('rows', 'sub')) + 1e-06  78.1 us
    all_gather x1, waiting for transfers between devices, complete_feature_rows(): return lax.all_gather(embeddings, 'sub', axis=1, tiled=True)  65.7 us
  transfers between devices with their start and end apart: 6, of which 6 were waited for; matrix products, arithmetic and copies ran while one was open for 0% of the time, Pallas kernels for 0%

commit v1 on v0

--- a/solution.py
+++ b/solution.py
@@ -62,7 +62,7 @@
     partial_value = lax.dot_general(
         full_x, rebuilt, (((0,), (1,)), ((), ())), preferred_element_type=jnp.float32
     )
-    summed = lax.psum(partial_value, "rows")
+    summed = jnp.sum(lax.all_gather(partial_value, axis_name="rows"), axis=0)
     own_cross = lax.dynamic_slice_in_dim(summed, lax.axis_index("rows") * row_share, row_share, 0)
     frob_norm = jnp.sqrt(lax.psum(jnp.sum(own_cross * own_cross), ("rows", "sub")) + 1e-06)
     polar_now = own_cross / frob_norm

time: 1480 us -> 1330 us (0.90)
  waiting for transfers between devices: 1030 us -> 856 us
  local copies, waits for them, and re-layouts: 1.74 us -> 19.6 us
    psum x1 -> x0, waiting for transfers between devices: 276 us -> none  [per_device(): summed = lax.psum(partial_value, 'rows')]
    all_gather x0 -> x1, waiting for transfers between devices: none -> 100 us  [per_device(): summed = jnp.sum(lax.all_gather(partial_value, axis_name='rows'), axis=0)]
    unnamed x8 -> x10, local copies, waits for them, and re-layouts: 0.3 us -> 18 us
where the time goes in v1:
time: 1330 us
  waiting for transfers between devices  856 us (64%)
  blocking collectives  395 us (30%)
  other arithmetic  23.4 us (2%)
  matrix products  23.4 us (2%)
  local copies, waits for them, and re-layouts  19.6 us (1%)
  between operations  15 us (1%)
    psum x2, waiting for transfers between devices, per_device(): totals, counts = lax.psum((totals, counts), 'rows')  500 us
    psum x2, waiting for transfers between devices, per_device(): gram_rows = lax.psum(gram_part, 'sub')  189 us
    psum x2, blocking collectives, per_device(): totals, counts = lax.psum((totals, counts), 'rows')  140 us
    all_gather x1, waiting for transfers between devices, per_device(): summed = jnp.sum(lax.all_gather(partial_value, axis_name='rows'), axis=0)  100 us
    all_gather x2, blocking collectives, per_device(): image_cols = lax.all_gather(image, 'rows', axis=0, tiled=True)  95.9 us
    all_gather x2, blocking collectives, per_device(): columns = lax.all_gather(polar_now, 'rows', axis=0, tiled=True)  81.7 us
    psum x1, blocking collectives, per_device(): lax.psum(jnp.sum(own_cross * own_cross), ('rows', 'sub')) + 1e-06  77.5 us
    all_gather x1, waiting for transfers between devices, complete_feature_rows(): return lax.all_gather(embeddings, 'sub', axis=1, tiled=True)  65.7 us
  transfers between devices with their start and end apart: 6, of which 6 were waited for; matrix products, arithmetic and copies ran while one was open for 0% of the time, Pallas kernels for 0%

profile of v1, /device:TPU:1, one launch (start us, length us, event | category | flops | bytes accessed | tf_op | source)
XLA Modules:
  0.0 1332.5 jit_solution(9058181554135349185)
XLA Ops:
  8.0 0.9 convert_element_type.30
  8.9 65.7 %all-gather.4.cloned.1.call-done = bf16[512,1024]{1,0:T(8,128)(2,1)} async-done(((bf16[512,128]{1,0:T(8,128)(2,1)}), bf16[512,1024]{1,0:T(8,128)(2,1)}) %all-gather.4.cloned.1.call-update) | async-done | bytes 1048592 | tf_op jit(solution)/shard_map/all_gather | solution.py:17
  74.6 1.7 convolution_convert_fusion.1
  76.4 12.3 while.26
  88.7 69.7 %psum.50 = f32[8,256]{1,0:T(8,128)S(1)} all-reduce(f32[8,256]{1,0:T(8,128)S(1)} %get-tuple-element.75), channel_id=1, replica_groups=mesh['rows'=32,'sub'=8] {'rows'}, use_global_device_ids=true, to_apply=%region_7.8 | all-reduce | flops 2048 | bytes 16384 | tf_op jit(solution)/shard_map/psum | solution.py:56
  158.5 247.6 %all-reduce.5.cloned.1.call-done = f32[8,16,256]{2,1,0:T(8,128)} async-done(((f32[8,16,256]{2,1,0:T(8,128)}), f32[8,16,256]{2,1,0:T(8,128)}) %all-reduce.5.cloned.1.call-update) | async-done | bytes 131088 | tf_op jit(solution)/shard_map/psum | solution.py:56
  406.1 1.0 fusion.27
  407.8 11.8 while.27
  408.3 0.8 fusion.72
  411.3 0.8 fusion.72
  412.7 0.8 fusion.72
  417.2 0.8 fusion.72
  419.7 70.0 %psum.52 = f32[8,256]{1,0:T(8,128)S(1)} all-reduce(f32[8,256]{1,0:T(8,128)S(1)} %get-tuple-element.77), channel_id=1, replica_groups=mesh['rows'=32,'sub'=8] {'rows'}, use_global_device_ids=true, to_apply=%region_15.16 | all-reduce | flops 2048 | bytes 16384 | tf_op jit(solution)/shard_map/psum | solution.py:56
  489.7 252.1 %all-reduce.7.cloned.1.call-done = f32[8,16,256]{2,1,0:T(8,128)} async-done(((f32[8,16,256]{2,1,0:T(8,128)}), f32[8,16,256]{2,1,0:T(8,128)}) %all-reduce.7.cloned.1.call-update) | async-done | bytes 131088 | tf_op jit(solution)/shard_map/psum | solution.py:56
  741.8 0.9 add_divide_fusion
  743.4 1.1 convolution_bitcast_fusion.2
  744.6 100.3 %all-gather.6.cloned.1.call-done = f32[32768,128]{0,1:T(8,128)} async-done(((f32[1024,128]{0,1:T(8,128)}), f32[32768,128]{0,1:T(8,128)}) %all-gather.6.cloned.1.call-update) | async-done | bytes 16777232 | tf_op jit(solution)/shard_map/all_gather | solution.py:65
  844.9 17.7 %copy.7 = f32[16,8,32,1024]{3,2,1,0:T(8,128)} copy(f32[16,8,32,1024]{3,1,2,0:T(8,128)} %bitcast.90) | data formatting | bytes 33554432
  862.6 9.0 bitcast_reduce_fusion
  872.4 77.5 %psum.53 = f32[]{:T(128)} all-reduce(f32[]{:T(128)} %multiply_reduce_fusion.2), channel_id=1, replica_groups=mesh['rows'=32,'sub'=8] {'rows','sub'}, use_global_device_ids=true, to_apply=%region_18.19 | all-reduce | flops 1 | bytes 8 | tf_op jit(solution)/shard_map/psum | solution.py:67
  950.6 42.4 %all_gather.24 = f32[1024,128]{1,0:T(8,128)S(1)} all-gather(f32[32,128]{1,0:T(8,128)S(1)} %broadcast_divide_fusion), channel_id=1, replica_groups=mesh['rows'=32,'sub'=8] {'rows'}, dimensions={0}, use_global_device_ids=true | all-gather | bytes 540672 | tf_op jit(solution)/shard_map/all_gather | solution.py:70
  993.0 1.3 fusion.30
  994.3 93.6 %all-reduce.9.cloned.1.call-done = f32[32,1024]{1,0:T(8,128)} async-done(((f32[32,1024]{1,0:T(8,128)}), f32[32,1024]{1,0:T(8,128)}) %all-reduce.9.cloned.1.call-update) | async-done | bytes 131088 | tf_op jit(solution)/shard_map/psum | solution.py:78
  1088.0 1.3 fusion.31
  1089.3 48.0 %all_gather.25 = f32[1024,128]{1,0:T(8,128)S(1)} all-gather(f32[32,128]{1,0:T(8,128)S(1)} %fusion.31), channel_id=1, replica_groups=mesh['rows'=32,'sub'=8] {'rows'}, dimensions={0}, use_global_device_ids=true | all-gather | bytes 540672 | tf_op jit(solution)/shard_map/all_gather | solution.py:82
  1137.3 1.3 fusion.25
  1138.6 39.3 %all_gather.26 = f32[1024,128]{1,0:T(8,128)S(1)} all-gather(f32[32,128]{1,0:T(8,128)S(1)} %fusion.25), channel_id=1, replica_groups=mesh['rows'=32,'sub'=8] {'rows'}, dimensions={0}, use_global_device_ids=true | all-gather | bytes 540672 | tf_op jit(solution)/shard_map/all_gather | solution.py:70
  1177.9 1.3 fusion.32
  1179.2 95.4 %all-reduce.11.cloned.1.call-done = f32[32,1024]{1,0:T(8,128)} async-done(((f32[32,1024]{1,0:T(8,128)}), f32[32,1024]{1,0:T(8,128)}) %all-reduce.11.cloned.1.call-update) | async-done | bytes 131088 | tf_op jit(solution)/shard_map/psum | solution.py:78
  1274.6 1.3 fusion.33
  1275.9 47.8 %all_gather.27 = f32[1024,128]{1,0:T(8,128)S(1)} all-gather(f32[32,128]{1,0:T(8,128)S(1)} %fusion.33), channel_id=1, replica_groups=mesh['rows'=32,'sub'=8] {'rows'}, dimensions={0}, use_global_device_ids=true | all-gather | bytes 540672 | tf_op jit(solution)/shard_map/all_gather | solution.py:82
  1323.7 1.9 fusion.24
  (132 shorter events, 23.6 us)
Async XLA Ops:
  7.2 67.5 %copy-start = (bf16[1024,128]{1,0:T(8,128)(2,1)S(1)}, bf16[1024,128]{1,0:T(8,128)(2,1)}, u32[]{:S(2)}) copy-start(bf16[1024,128]{1,0:T(8,128)(2,1)} %param.8) | copy-start | bytes 786436
  7.2 67.5 %all-gather.4.cloned.1.call-start = ((), (), s32[]{:S(2)}) async-start(), calls=%async_computation | async-start | bytes 1179648 | tf_op jit(solution)/shard_map/all_gather | solution.py:17
  7.9 398.2 %all-reduce.5.cloned.1.call-start = ((), (), s32[]{:S(2)}) async-start(), calls=%async_computation.1 | async-start | bytes 262144 | tf_op jit(solution)/shard_map/psum | solution.py:56
  88.7 69.7 %copy-start.3 = (f32[8,16,256]{2,1,0:T(8,128)}, f32[8,16,256]{2,1,0:T(8,128)S(1)}, u32[]{:S(2)}) copy-start(f32[8,16,256]{2,1,0:T(8,128)S(1)} %get-tuple-element.74) | copy-start | bytes 393220
  158.5 583.4 %all-reduce.7.cloned.1.call-start = ((), (), s32[]{:S(2)}) async-start(), calls=%async_computation.2 | async-start | bytes 262144 | tf_op jit(solution)/shard_map/psum | solution.py:56
  419.6 323.8 %copy-start.1 = (bf16[512,1024]{1,0:T(8,128)(2,1)S(1)}, bf16[512,1024]{1,0:T(8,128)(2,1)}, u32[]{:S(2)}) copy-start(bf16[512,1024]{1,0:T(8,128)(2,1)} %all-gather.4.cloned.1.call-done) | copy-start | bytes 3145732
  489.7 355.3 %all-gather.6.cloned.1.call-start = ((), (), s32[]{:S(2)}) async-start(), calls=%async_computation.5 | async-start | bytes 17301504 | tf_op jit(solution)/shard_map/all_gather | solution.py:65
  742.8 0.7 copy-start.2
  744.5 343.4 %all-reduce.9.cloned.1.call-start = ((), (), s32[]{:S(2)}) async-start(), calls=%async_computation.3 | async-start | bytes 262144 | tf_op jit(solution)/shard_map/psum | solution.py:78
  994.3 280.3 %all-reduce.11.cloned.1.call-start = ((), (), s32[]{:S(2)}) async-start(), calls=%async_computation.4 | async-start | bytes 262144 | tf_op jit(solution)/shard_map/psum | solution.py:78
Sparse Core Ops, SparseCore 0:
  10.5 64.1 all-gather.3
  158.6 247.4 all-reduce.4
  489.8 251.9 all-reduce.6
  744.7 100.2 all-gather.5
  994.4 93.5 all-reduce.8
  1179.3 95.2 all-reduce.10
